TPU v7x, 32 devices: a whole 2x2x4 slice. The times are simulated.
32 devices in a mesh: ep: 8 (over z, x), tp: 4 (over y, core).
Axes of the slice: x: 2, y: 2, z: 4, core: 2. Of those that a mesh axis runs over, the one named last changes fastest.
Arguments:
- hidden_in: bfloat16 [1024, 2048], P('ep', 'tp'), may hold values from -6 to 6
- norm_gain: float32 [2048], replicated, may hold values from 0.5 to 1.5
- router_weight: bfloat16 [2048, 8], replicated, may hold values from -4.861359 to 4.861359
- shared_gate_up: bfloat16 [2048, 2, 1408], P(None, None, 'tp'), may hold values from -0.125 to 0.125
- shared_down: bfloat16 [1408, 2048], P('tp'), may hold values from -0.15625 to 0.15625
- slot_gate_up: bfloat16 [32, 2048, 2, 704], P(('ep', 'tp')), as said below
- slot_down: bfloat16 [32, 704, 2048], P(('ep', 'tp')), as said below
- slot_expert: int32 [32], replicated, may hold values from 0 to 7, as said below
- slot_choice: int32 [1024, 6], P('ep'), may hold values from 0 to 31, all different within a row; in each aligned block of 32 rows (0 to 31, 32 to 63, ...) at most 12 rows name the same one
- live_count: int32 [8], P('ep'), may hold values from 64 to 128, as said below
Outputs:
- mixed_out: bfloat16 [1024, 2048], P('ep', 'tp')
Inputs may be any that keep to these rules, and one draw needn't show every extreme that they name: `slot_expert`: each expert is held by 1 or 7 slots; exactly 4 experts by the larger number. `slot_gate_up`: entry s holds the weights of expert slot_expert[s]; slots of one expert hold equal weights. `slot_down`: entry s holds the weights of expert slot_expert[s]; slots of one expert hold equal weights. `slot_choice`: a row names 6 different slots; in each aligned block of 32 rows no slot is named more than 12 times. `live_count`: the live rows of an index of ep are its first ones; some index of ep has all 128 rows live.
All inputs are finite; a program needn't handle non-finite values.
Results may differ from a plain program's by a relative error of at most 0.0058.
Values may be sent and summed in bfloat16 or wider, within the bound.
A program may use at most 64 MiB of HBM per device.

v0:
```python
import jax
import jax.numpy as jnp
from jax import lax
from jax.sharding import PartitionSpec as P


def gate_weights(normed_rows, choices, router_weight, slot_expert):
    logits = jnp.dot(normed_rows, router_weight, preferred_element_type=jnp.float32)
    slot_total = slot_expert.shape[0]
    expert_total = router_weight.shape[1]
    slot_hit = choices[:, :, None] == jnp.arange(slot_total, dtype=jnp.int32)
    expert_ids = jnp.sum(jnp.where(slot_hit, slot_expert, 0), axis=2)
    expert_hit = expert_ids[:, :, None] == jnp.arange(expert_total, dtype=jnp.int32)
    picked = jnp.sum(jnp.where(expert_hit, logits[:, None, :], 0.0), axis=2)
    highest = jnp.max(picked, axis=1, keepdims=True)
    weights = jnp.exp(picked - highest)
    return (weights / jnp.sum(weights, axis=1, keepdims=True)).astype(jnp.bfloat16)


def slot_positions(targets):
    length = targets.shape[0]
    same_slot = targets[:, None] == targets[None, :]
    earlier = jnp.arange(length)[None, :] < jnp.arange(length)[:, None]
    return jnp.sum(same_slot & earlier, axis=1)


def expert_apply(received, slot_gate_up, slot_down):
    shape_in = received.shape
    flat_rows = received.reshape(-1, shape_in[-1])
    gate_up = jnp.einsum(
        "rd,dgf->rgf", flat_rows, slot_gate_up[0], preferred_element_type=jnp.float32
    )
    activated = (jax.nn.silu(gate_up[:, 0]) * gate_up[:, 1]).astype(jnp.bfloat16)
    result = jnp.dot(activated, slot_down[0], preferred_element_type=jnp.float32).astype(
        jnp.bfloat16
    )
    return result.reshape(shape_in)


def local(
    hidden_in,
    norm_gain,
    router_weight,
    shared_gate_up,
    shared_down,
    slot_gate_up,
    slot_down,
    slot_expert,
    slot_choice,
    live_count,
):
    tp_count = lax.axis_size("tp")
    ep_count = lax.axis_size("ep")
    tp_index = lax.axis_index("tp")
    tok_count = hidden_in.shape[0]
    feature_width = hidden_in.shape[1] * tp_count
    top_count = slot_choice.shape[1]
    slot_count = slot_expert.shape[0]
    quarter = tok_count // tp_count
    capacity = max(2, 2 * quarter * top_count // slot_count)
    full_rows = lax.all_gather(hidden_in, "tp", axis=1, tiled=True)
    wide_rows = full_rows.astype(jnp.float32)
    norm_scale = lax.rsqrt(jnp.mean(wide_rows * wide_rows, axis=1, keepdims=True) + 1e-06)
    normed = (wide_rows * norm_scale * norm_gain).astype(jnp.bfloat16)
    shared_proj = jnp.einsum(
        "td,dgf->tgf", normed, shared_gate_up, preferred_element_type=jnp.float32
    )
    shared_hidden = (jax.nn.silu(shared_proj[:, 0]) * shared_proj[:, 1]).astype(jnp.bfloat16)
    partial_value = jnp.dot(shared_hidden, shared_down, preferred_element_type=jnp.float32)
    row_start = tp_index * quarter
    own_rows = lax.dynamic_slice_in_dim(normed, row_start, quarter, 0)
    own_choice = lax.dynamic_slice_in_dim(slot_choice, row_start, quarter, 0)
    gate_values = gate_weights(own_rows, own_choice, router_weight, slot_expert)
    targets = own_choice.reshape(-1)
    placed = targets * capacity + slot_positions(targets)
    outgoing = jnp.zeros((slot_count * capacity, feature_width), jnp.bfloat16)
    outgoing = outgoing.at[placed].set(jnp.repeat(own_rows, top_count, axis=0))
    outgoing = outgoing.reshape(ep_count, tp_count, capacity, feature_width)
    arrived = lax.all_to_all(
        lax.all_to_all(outgoing, "ep", split_axis=0, concat_axis=0, tiled=True),
        "tp",
        split_axis=1,
        concat_axis=1,
        tiled=True,
    )
    computed = expert_apply(arrived, slot_gate_up, slot_down)
    returned = lax.all_to_all(
        lax.all_to_all(computed, "ep", split_axis=0, concat_axis=0, tiled=True),
        "tp",
        split_axis=1,
        concat_axis=1,
        tiled=True,
    )
    fetched = returned.reshape(-1, feature_width)[placed].reshape(quarter, top_count, feature_width)
    routed = jnp.einsum("qk,qkd->qd", gate_values, fetched, preferred_element_type=jnp.float32)
    own_partial = lax.dynamic_slice_in_dim(partial_value, row_start, quarter, 0) + routed
    partial_value = lax.dynamic_update_slice_in_dim(partial_value, own_partial, row_start, 0)
    summed = lax.psum_scatter(partial_value, "tp", scatter_dimension=1, tiled=True)
    live_rows = jnp.arange(tok_count, dtype=jnp.int32) < live_count[0]
    mixed_out = jnp.where(live_rows[:, None], hidden_in.astype(jnp.float32) + summed, 0.0)
    return mixed_out.astype(jnp.bfloat16)


def solution(mesh):
    in_specs = (
        P("ep", "tp"),
        P(),
        P(),
        P(None, None, "tp"),
        P("tp", None),
        P(("ep", "tp"), None, None, None),
        P(("ep", "tp"), None, None),
        P(),
        P("ep", None),
        P("ep"),
    )
    out_specs = P("ep", "tp")
    return jax.shard_map(local, mesh=mesh, in_specs=in_specs, out_specs=out_specs, check_vma=False)
```

profile of v0, /device:TPU:0, one launch (start us, length us, event | category | flops | bytes accessed | tf_op | source)
XLA Modules:
  0.0 238.2 jit_solution(8258291260687447549)
XLA Ops:
  6.5 9.0 %all_gather.3 = bf16[128,2048]{1,0:T(8,128)(2,1)S(1)} all-gather(bf16[128,512]{1,0:T(8,128)(2,1)} %param.10), channel_id=1, replica_groups=mesh['ep'=8,'tp'=4] {'tp'}, dimensions={1}, use_global_device_ids=true | all-gather | bytes 655360 | tf_op jit(solution)/shard_map/all_gather | solution.py:61
  15.7 0.9 fusion.10
  16.6 0.8 copy-done.1
  18.1 1.1 broadcast_in_dim.58
  19.2 2.2 reshape.86
  21.4 3.7 %scatter_custom_fusion = bf16[384,2048]{1,0:T(8,128)(2,1)} fusion(s32[192]{0:T(256)S(1)} %bitcast.43, bf16[192,2048]{1,0:T(8,128)(2,1)} %reshape.86, bf16[]{:T(256)} %constant.10.clone.1), kind=kCustom, calls=%fused_computation.14 | custom fusion | bytes 1573376 | tf_op jit(solution)/shard_map/scatter | solution.py:77
  25.1 3.6 %reshape.69 = bf16[8,4,12,2048]{3,2,1,0:T(8,128)(2,1)} reshape(bf16[384,2048]{1,0:T(8,128)(2,1)} %scatter_custom_fusion) | data formatting | bytes 3145728 | tf_op jit(solution)/shard_map/reshape | solution.py:78
  28.7 2.8 %copy.29 = bf16[8,4,12,2048]{3,1,2,0:T(4,128)(2,1)S(1)} copy(bf16[8,4,12,2048]{3,2,1,0:T(8,128)(2,1)} %reshape.69) | data formatting | bytes 3145728 | tf_op jit(solution)/shard_map/reshape | solution.py:78
  31.5 43.1 %all_to_all.20 = bf16[8,4,12,2048]{3,1,2,0:T(4,128)(2,1)S(1)} all-to-all(bf16[8,4,12,2048]{3,1,2,0:T(4,128)(2,1)S(1)} %copy.29), channel_id=1, replica_groups=mesh['ep'=8,'tp'=4] {'ep'}, dimensions={0} | all-to-all | bytes 3145728 | tf_op jit(solution)/shard_map/all_to_all | solution.py:80
  74.6 0.9 copy.30
  75.5 22.5 %all_to_all.21 = bf16[8,4,12,2048]{3,0,2,1:T(8,128)(2,1)S(1)} all-to-all(bf16[8,4,12,2048]{3,0,2,1:T(8,128)(2,1)S(1)} %copy.30), channel_id=1, replica_groups=mesh['ep'=8,'tp'=4] {'tp'}, dimensions={1} | all-to-all | bytes 3145728 | tf_op jit(solution)/shard_map/all_to_all | solution.py:79
  98.0 2.2 copy.31
  100.3 3.6 %reshape.91 = bf16[384,2048,1]{1,0,2:T(8,128)(2,1)} reshape(bf16[8,4,12,2048]{3,2,1,0:T(8,128)(2,1)} %copy.31) | data formatting | bytes 3145728 | tf_op jit(solution)/shard_map/reshape | solution.py:29
  103.9 5.6 %fusion = f32[384,2,704]{0,2,1:T(8,128)S(1)} fusion(bf16[384,2048,1]{1,0,2:T(8,128)(2,1)} %reshape.91, bf16[1,2048,2,704]{1,3,2,0:T(8,128)(2,1)} %param.15), kind=kOutput, calls=%fused_computation.2 | convolution fusion | flops 2214592512 | bytes 9502720 | tf_op jit(solution)/shard_map/rd,dgf->rgf/dot_general | solution.py:30
  109.5 2.6 %fusion.4 = bf16[384,2048]{1,0:T(8,128)(2,1)} fusion(bf16[1,704,2048]{2,1,0:T(8,128)(2,1)S(1)} %copy-done, f32[384,2,704]{0,2,1:T(8,128)S(1)} %fusion), kind=kOutput, calls=%fused_computation.6 | convolution fusion | flops 1109704704 | bytes 6619136 | tf_op jit(solution)/shard_map/dot_general | solution.py:34
  112.2 3.6 %reshape.71 = bf16[8,4,12,2048]{3,2,1,0:T(8,128)(2,1)} reshape(bf16[384,2048]{1,0:T(8,128)(2,1)} %fusion.4) | data formatting | bytes 3145728 | tf_op jit(solution)/shard_map/reshape | solution.py:37
  115.8 4.0 %copy.32 = bf16[8,4,12,2048]{3,1,2,0:T(4,128)(2,1)} copy(bf16[8,4,12,2048]{3,2,1,0:T(8,128)(2,1)} %reshape.71) | data formatting | bytes 3145728 | tf_op jit(solution)/shard_map/reshape | solution.py:37
  119.7 4.6 %all-to-all-start.2 = ((bf16[8,4,12,2048]{3,1,2,0:T(4,128)(2,1)}), bf16[8,4,12,2048]{3,1,2,0:T(4,128)(2,1)}, u32[]{:S(2)}, u32[]{:S(2)}) async-start(bf16[8,4,12,2048]{3,1,2,0:T(4,128)(2,1)} %copy.32), calls=%async_computation.2 | async-start | bytes 3145728 | tf_op jit(solution)/shard_map/all_to_all | solution.py:88
  124.5 36.6 %all-to-all-done.2 = bf16[8,4,12,2048]{3,1,2,0:T(4,128)(2,1)} async-done(((bf16[8,4,12,2048]{3,1,2,0:T(4,128)(2,1)}), bf16[8,4,12,2048]{3,1,2,0:T(4,128)(2,1)}, u32[]{:S(2)}, u32[]{:S(2)}) %all-to-all-start.2) | async-done | bytes 1572896 | tf_op jit(solution)/shard_map/all_to_all | solution.py:88
  161.1 3.4 %copy.33 = bf16[8,4,12,2048]{3,0,2,1:T(8,128)(2,1)} copy(bf16[8,4,12,2048]{3,1,2,0:T(4,128)(2,1)} %all-to-all-done.2) | data formatting | bytes 3145728 | tf_op jit(solution)/shard_map/all_to_all | solution.py:88
  164.5 4.5 %all-to-all-start.3 = ((bf16[8,4,12,2048]{3,0,2,1:T(8,128)(2,1)}), bf16[8,4,12,2048]{3,0,2,1:T(8,128)(2,1)}, u32[]{:S(2)}, u32[]{:S(2)}) async-start(bf16[8,4,12,2048]{3,0,2,1:T(8,128)(2,1)} %copy.33), calls=%async_computation.3 | async-start | bytes 3145728 | tf_op jit(solution)/shard_map/all_to_all | solution.py:87
  169.5 2.8 %fusion.15 = f32[128,2,352]{0,2,1:T(8,128)S(1)} fusion(bf16[2048,2,352]{0,2,1:T(8,128)(2,1)} %param.13, bf16[128,2048]{1,0:T(8,128)(2,1)S(1)} %copy-done.2), kind=kOutput, calls=%fused_computation.17 | convolution fusion | flops 369098752 | bytes 3768320 | tf_op jit(solution)/shard_map/td,dgf->tgf/dot_general | solution.py:65
  172.4 1.5 fusion.21
  173.9 15.2 %all-to-all-done.3 = bf16[8,4,12,2048]{3,0,2,1:T(8,128)(2,1)} async-done(((bf16[8,4,12,2048]{3,0,2,1:T(8,128)(2,1)}), bf16[8,4,12,2048]{3,0,2,1:T(8,128)(2,1)}, u32[]{:S(2)}, u32[]{:S(2)}) %all-to-all-start.3) | async-done | bytes 1572896 | tf_op jit(solution)/shard_map/all_to_all | solution.py:87
  189.1 3.6 %copy.34 = bf16[8,4,12,2048]{3,2,1,0:T(8,128)(2,1)} copy(bf16[8,4,12,2048]{3,0,2,1:T(8,128)(2,1)} %all-to-all-done.3) | data formatting | bytes 3145728 | tf_op jit(solution)/shard_map/all_to_all | solution.py:87
  192.8 3.6 %reshape.72 = bf16[384,2048]{1,0:T(8,128)(2,1)} reshape(bf16[8,4,12,2048]{3,2,1,0:T(8,128)(2,1)} %copy.34) | data formatting | bytes 3145728 | tf_op jit(solution)/shard_map/reshape | solution.py:94
  196.4 4.4 %gather_fusion = bf16[192,2048]{1,0:T(8,128)(2,1)} fusion(bf16[384,2048]{1,0:T(8,128)(2,1)} %reshape.72, s32[1024]{0:T(1024)S(1)} %pad_clamp_fusion), kind=kCustom, calls=%fused_computation | custom fusion | bytes 1573632 | tf_op jit(solution)/shard_map/gather | solution.py:94
  200.8 2.2 reshape.73
  203.0 1.7 fusion.29
  204.7 1.7 fusion.17
  207.1 22.5 %reduce-scatter.2.cloned.1.call-done = f32[128,512]{1,0:T(8,128)} async-done(((f32[128,2048]{1,0:T(8,128)}), f32[128,512]{1,0:T(8,128)}) %reduce-scatter.2.cloned.1.call-update) | async-done | bytes 262160 | tf_op jit(solution)/shard_map/reduce_scatter | solution.py:98
  229.6 1.7 select_convert_fusion
  (36 shorter events, 1.5 us)
Async XLA Ops:
  6.5 103.0 %copy-start = (bf16[1,704,2048]{2,1,0:T(8,128)(2,1)S(1)}, bf16[1,704,2048]{2,1,0:T(8,128)(2,1)}, u32[]{:S(2)}) copy-start(bf16[1,704,2048]{2,1,0:T(8,128)(2,1)} %param.16) | copy-start | bytes 8650756
  6.5 10.9 %copy-start.6 = (s32[128,6]{0,1:T(8,128)S(1)}, s32[128,6]{0,1:T(8,128)}, u32[]{:S(2)}) copy-start(s32[128,6]{0,1:T(8,128)} %param.18) | copy-start | bytes 9220
  16.6 0.8 copy-start.1
  119.7 4.6 %copy-start.5 = (bf16[2048,8]{0,1:T(8,128)(2,1)S(1)}, bf16[2048,8]{0,1:T(8,128)(2,1)}, u32[]{:S(2)}) copy-start(bf16[2048,8]{0,1:T(8,128)(2,1)} %param.12) | copy-start | bytes 98308
  119.7 41.3 %all-to-all-start.2 = ((bf16[8,4,12,2048]{3,1,2,0:T(4,128)(2,1)}), bf16[8,4,12,2048]{3,1,2,0:T(4,128)(2,1)}, u32[]{:S(2)}, u32[]{:S(2)}) async-start(bf16[8,4,12,2048]{3,1,2,0:T(4,128)(2,1)} %copy.32), calls=%async_computation.2 | async-start | bytes 3145728 | tf_op jit(solution)/shard_map/all_to_all | solution.py:88
  164.5 4.5 %copy-start.7 = (s32[32]{0:T(128)S(1)}, s32[32]{0:T(128)}, u32[]{:S(2)}) copy-start(s32[32]{0:T(128)} %param.17) | copy-start | bytes 388
  164.5 5.0 %copy-start.2 = (bf16[128,2048]{1,0:T(8,128)(2,1)S(1)}, bf16[128,2048]{1,0:T(8,128)(2,1)}, u32[]{:S(2)}) copy-start(bf16[128,2048]{1,0:T(8,128)(2,1)} %copy-done.1) | copy-start | bytes 1572868
  164.5 24.6 %all-to-all-start.3 = ((bf16[8,4,12,2048]{3,0,2,1:T(8,128)(2,1)}), bf16[8,4,12,2048]{3,0,2,1:T(8,128)(2,1)}, u32[]{:S(2)}, u32[]{:S(2)}) async-start(bf16[8,4,12,2048]{3,0,2,1:T(8,128)(2,1)} %copy.33), calls=%async_computation.3 | async-start | bytes 3145728 | tf_op jit(solution)/shard_map/all_to_all | solution.py:87
  169.0 60.6 %reduce-scatter.2.cloned.1.call-start = ((), (), s32[]{:S(2)}) async-start(), calls=%async_computation.5 | async-start | bytes 1310720 | tf_op jit(solution)/shard_map/reduce_scatter | solution.py:98
  169.5 2.9 %copy-start.3 = (bf16[352,2048]{1,0:T(8,128)(2,1)S(1)}, bf16[352,2048]{1,0:T(8,128)(2,1)}, u32[]{:S(2)}) copy-start(bf16[352,2048]{1,0:T(8,128)(2,1)} %param.14) | copy-start | bytes 4325380
  203.0 26.6 %copy-start.4 = (bf16[128,512]{1,0:T(8,128)(2,1)S(1)}, bf16[128,512]{1,0:T(8,128)(2,1)}, u32[]{:S(2)}) copy-start(bf16[128,512]{1,0:T(8,128)(2,1)} %param.10) | copy-start | bytes 393220
Sparse Core Ops, SparseCore 0:
  206.6 22.9 reduce-scatter.1
where the time goes:
time: 239 us; the launch traced here: 238 us
  blocking collectives  74.6 us (31%)
  waiting for transfers between devices  74.3 us (31%)
  local copies, waits for them, and re-layouts  46.3 us (19%)
  matrix products  14.5 us (6%)
  between operations  14.2 us (6%)
  starting transfers between devices  9.12 us (4%)
  other arithmetic  5.13 us (2%)
    all_to_all x1, blocking collectives, local(): lax.all_to_all(outgoing, 'ep', split_axis=0, concat_axis=0, tiled=True)  43.1 us
    all_to_all x1, waiting for transfers between devices, local(): lax.all_to_all(computed, 'ep', split_axis=0, concat_axis=0, tiled=True)  36.6 us
    all_to_all x1, blocking collectives, local(): lax.all_to_all(lax.all_to_all(outgoing, 'ep', split_axis=0, concat_axis=0...  22.5 us
    reduce_scatter x1, waiting for transfers between devices, local(): lax.psum_scatter(partial_value, 'tp', scatter_dimension=1, tiled=True)  22.5 us
    all_to_all x1, waiting for transfers between devices, local(): lax.all_to_all(lax.all_to_all(computed, 'ep', split_axis=0, concat_axis=0...  15.2 us
    all_gather x1, blocking collectives, local(): full_rows = lax.all_gather(hidden_in, 'tp', axis=1, tiled=True)  8.98 us
    reshape x2, local copies, waits for them, and re-layouts, expert_apply(): return result.reshape(shape_in)  7.55 us
    reshape x2, local copies, waits for them, and re-layouts, local(): outgoing = outgoing.reshape(ep_count, tp_count, capacity, feature_width)  6.42 us
  transfers between devices with their start and end apart: 3, of which 3 were waited for; matrix products, arithmetic and copies ran while one was open for 2% of the time, Pallas kernels for 0%

commit v1 on v0

--- a/solution.py
+++ b/solution.py
@@ -2,6 +2,29 @@
 import jax.numpy as jnp
 from jax import lax
 from jax.sharding import PartitionSpec as P
+
+
+def split_up(x, dim, peers):
+    lengths = x.shape
+    tiles = x.reshape(*lengths[:dim], peers, lengths[dim] // peers, *lengths[dim + 1 :])
+    return jnp.moveaxis(tiles, dim, 0)
+
+
+def in_order(parts, dim):
+    parts = jnp.moveaxis(parts, 0, dim)
+    lengths = parts.shape
+    return parts.reshape(*lengths[:dim], lengths[dim] * lengths[dim + 1], *lengths[dim + 2 :])
+
+
+def exchange_in_pairs(array, axis, split_dim, concat_dim):
+    size, index = (lax.axis_size(axis), lax.axis_index(axis))
+    tiles = split_up(array, split_dim, size)
+    done = [tiles[index]]
+    for lap in range(1, size):
+        sent = tiles[index ^ lap]
+        done.append(lax.ppermute(sent, axis, [(i, i ^ lap) for i in range(size)]))
+    tiles = jnp.stack(done)[index ^ jnp.arange(size)]
+    return in_order(tiles, concat_dim)
 
 
 def gate_weights(normed_rows, choices, router_weight, slot_expert):
@@ -77,11 +100,7 @@
     outgoing = outgoing.at[placed].set(jnp.repeat(own_rows, top_count, axis=0))
     outgoing = outgoing.reshape(ep_count, tp_count, capacity, feature_width)
     arrived = lax.all_to_all(
-        lax.all_to_all(outgoing, "ep", split_axis=0, concat_axis=0, tiled=True),
-        "tp",
-        split_axis=1,
-        concat_axis=1,
-        tiled=True,
+        exchange_in_pairs(outgoing, "ep", 0, 0), "tp", split_axis=1, concat_axis=1, tiled=True
     )
     computed = expert_apply(arrived, slot_gate_up, slot_down)
     returned = lax.all_to_all(

time: 239 us -> 253 us (1.059)
  blocking collectives: 74.6 us -> 31.4 us
  waiting for transfers between devices: 74.3 us -> 101 us
  starting transfers between devices: 9.12 us -> 28.7 us
  local copies, waits for them, and re-layouts: 46.3 us -> 55.5 us
    all_to_all x2 -> x1, blocking collectives: 65.6 us -> 22.5 us  [local(): lax.all_to_all(exchange_in_pairs(outgoing, 'ep', 0, 0), 'tp', split_axis=...]
    ppermute x0 -> x7, waiting for transfers between devices: none -> 27.8 us  [exchange_in_pairs(): done.append(lax.ppermute(sent, axis, [(i, i ^ lap) for i in range(size)]))]
    ppermute x0 -> x7, starting transfers between devices: none -> 11.9 us  [exchange_in_pairs(): done.append(lax.ppermute(sent, axis, [(i, i ^ lap) for i in range(size)]))]
    all_to_all x1, starting transfers between devices: 4.6 us -> 12.3 us  [local(): lax.all_to_all(computed, 'ep', split_axis=0, concat_axis=0, tiled=True)]
    reshape x2 -> x0, local copies, waits for them, and re-layouts: 6.42 us -> none  [local(): outgoing = outgoing.reshape(ep_count, tp_count, capacity, feature_width)]
    gather x0 -> x2, local copies, waits for them, and re-layouts: none -> 6.08 us  [exchange_in_pairs(): tiles = jnp.stack(done)[index ^ jnp.arange(size)]]
    another operation x0 -> x2, local copies, waits for them, and re-layouts: none -> 4.33 us  [the longest x1 3.6 us: split_up(): x.reshape(*lengths[:dim], peers, lengths[dim] // peers, *lengths[dim + 1:])]
    unnamed x16 -> x14, local copies, waits for them, and re-layouts: 0.81 us -> 4.37 us
  transfers between devices with their start and end apart: 3 -> 10, of which waited for: 3 -> 7; matrix products, arithmetic and copies ran while one was open for 2% -> 4% of each run, Pallas kernels for 0% -> 0%
where the time goes in v1:
time: 253 us; the launch traced here: 252 us
  waiting for transfers between devices  101 us (40%)
  local copies, waits for them, and re-layouts  55.5 us (22%)
  blocking collectives  31.4 us (12%)
  starting transfers between devices  28.7 us (11%)
  matrix products  15.2 us (6%)
  between operations  14.2 us (6%)
  other arithmetic  5.98 us (2%)
    all_to_all x1, waiting for transfers between devices, local(): lax.all_to_all(computed, 'ep', split_axis=0, concat_axis=0, tiled=True)  36.9 us
    ppermute x7, waiting for transfers between devices, exchange_in_pairs(): done.append(lax.ppermute(sent, axis, [(i, i ^ lap) for i in range(size)]))  27.8 us
    all_to_all x1, blocking collectives, local(): lax.all_to_all(exchange_in_pairs(outgoing, 'ep', 0, 0), 'tp', split_axis=...  22.5 us
    reduce_scatter x1, waiting for transfers between devices, local(): lax.psum_scatter(partial_value, 'tp', scatter_dimension=1, tiled=True)  21.5 us
    all_to_all x1, waiting for transfers between devices, local(): lax.all_to_all(lax.all_to_all(computed, 'ep', split_axis=0, concat_axis=0...  15.3 us
    all_to_all x1, starting transfers between devices, local(): lax.all_to_all(computed, 'ep', split_axis=0, concat_axis=0, tiled=True)  12.3 us
    ppermute x7, starting transfers between devices, exchange_in_pairs(): done.append(lax.ppermute(sent, axis, [(i, i ^ lap) for i in range(size)]))  11.9 us
    all_gather x1, blocking collectives, local(): full_rows = lax.all_gather(hidden_in, 'tp', axis=1, tiled=True)  8.86 us
  transfers between devices with their start and end apart: 10, of which 7 were waited for; matrix products, arithmetic and copies ran while one was open for 4% of the time, Pallas kernels for 0%

profile of v1, /device:TPU:0, one launch (start us, length us, event | category | flops | bytes accessed | tf_op | source)
XLA Modules:
  0.0 252.3 jit_solution(1723008322980112782)
XLA Ops:
  8.0 8.9 %all_gather.3 = bf16[128,2048]{1,0:T(8,128)(2,1)S(1)} all-gather(bf16[128,512]{1,0:T(8,128)(2,1)} %param.10), channel_id=1, replica_groups=mesh['ep'=8,'tp'=4] {'tp'}, dimensions={1}, use_global_device_ids=true | all-gather | bytes 655360 | tf_op jit(solution)/shard_map/all_gather | solution.py:84
  19.2 2.2 reshape.112
  21.3 3.7 %scatter_custom_fusion = bf16[384,2048]{1,0:T(8,128)(2,1)} fusion(s32[192]{0:T(256)S(1)} %bitcast.74, bf16[192,2048]{1,0:T(8,128)(2,1)} %reshape.112, bf16[]{:T(256)} %constant.11.clone.1), kind=kCustom, calls=%fused_computation.15 | custom fusion | bytes 1573376 | tf_op jit(solution)/shard_map/scatter | solution.py:100
  25.0 3.6 %reshape_reshape.3 = bf16[8,1,4,12,2048]{4,3,2,0,1:T(8,128)(2,1)} reshape(bf16[384,2048]{1,0:T(8,128)(2,1)} %scatter_custom_fusion) | data formatting | bytes 3145728 | tf_op jit(solution)/shard_map/reshape;reshape | solution.py:9
  28.6 2.4 dynamic-slice_bitcast_fusion
  34.5 2.6 %collective-permute-start.3 = (bf16[1,4,12,2048]{3,2,1,0:T(8,128)(2,1)S(1)}, bf16[1,4,12,2048]{3,2,1,0:T(8,128)(2,1)S(1)}, u32[]{:S(2)}, u32[]{:S(2)}) collective-permute-start(bf16[1,4,12,2048]{3,2,1,0:T(8,128)(2,1)S(1)} %get-tuple-element.10), channel_id=1, source_target_pairs={{0,16},{4,20},{8,24},{12,28},{16,0},{20,4},{24,8},{28,12},{1,17},{... | collective-permute-start | bytes 589832 | tf_op jit(solution)/shard_map/ppermute | solution.py:25
  39.6 3.6 %collective-permute-start.5 = (bf16[1,4,12,2048]{3,2,1,0:T(8,128)(2,1)S(1)}, bf16[1,4,12,2048]{3,2,1,0:T(8,128)(2,1)S(1)}, u32[]{:S(2)}, u32[]{:S(2)}) collective-permute-start(bf16[1,4,12,2048]{3,2,1,0:T(8,128)(2,1)S(1)} %get-tuple-element.8), channel_id=1, source_target_pairs={{0,24},{4,28},{8,16},{12,20},{16,8},{20,12},{24,0},{28,4},{1,25},{... | collective-permute-start | bytes 589832 | tf_op jit(solution)/shard_map/ppermute | solution.py:25
  43.9 8.1 %collective-permute-done.1 = bf16[1,4,12,2048]{3,2,1,0:T(8,128)(2,1)S(1)} collective-permute-done((bf16[1,4,12,2048]{3,2,1,0:T(8,128)(2,1)S(1)}, bf16[1,4,12,2048]{3,2,1,0:T(8,128)(2,1)S(1)}, u32[]{:S(2)}, u32[]{:S(2)}) %collective-permute-start.1) | collective-permute-done | bytes 196640 | tf_op jit(solution)/shard_map/ppermute | solution.py:25
  53.7 2.5 %collective-permute-done.2 = bf16[1,4,12,2048]{3,2,1,0:T(8,128)(2,1)S(1)} collective-permute-done((bf16[1,4,12,2048]{3,2,1,0:T(8,128)(2,1)S(1)}, bf16[1,4,12,2048]{3,2,1,0:T(8,128)(2,1)S(1)}, u32[]{:S(2)}, u32[]{:S(2)}) %collective-permute-start.2) | collective-permute-done | bytes 196640 | tf_op jit(solution)/shard_map/ppermute | solution.py:25
  57.7 15.9 %collective-permute-done.4 = bf16[1,4,12,2048]{3,2,1,0:T(8,128)(2,1)S(1)} collective-permute-done((bf16[1,4,12,2048]{3,2,1,0:T(8,128)(2,1)S(1)}, bf16[1,4,12,2048]{3,2,1,0:T(8,128)(2,1)S(1)}, u32[]{:S(2)}, u32[]{:S(2)}) %collective-permute-start.4) | collective-permute-done | bytes 196640 | tf_op jit(solution)/shard_map/ppermute | solution.py:25
  75.8 3.6 %gather_fusion = bf16[8,4,12,2048]{3,2,1,0:T(8,128)(2,1)} fusion(bf16[8,4,12,2048]{3,2,1,0:T(8,128)(2,1)} %bitcast.21, s32[1024]{0:T(1024)S(1)} %pad_clamp_fusion.1), kind=kCustom, calls=%fused_computation | custom fusion | bytes 3145760 | tf_op jit(solution)/shard_map/gather | solution.py:26
  79.5 2.5 copy.28
  81.9 22.5 %all_to_all.15 = bf16[8,4,12,2048]{3,0,2,1:T(8,128)(2,1)S(1)} all-to-all(bf16[8,4,12,2048]{3,0,2,1:T(8,128)(2,1)S(1)} %copy.28), channel_id=1, replica_groups=mesh['ep'=8,'tp'=4] {'tp'}, dimensions={1} | all-to-all | bytes 3145728 | tf_op jit(solution)/shard_map/all_to_all | solution.py:102
  104.4 2.2 copy.29
  106.7 3.6 %reshape.118 = bf16[384,2048,1]{1,0,2:T(8,128)(2,1)} reshape(bf16[8,4,12,2048]{3,2,1,0:T(8,128)(2,1)} %copy.29) | data formatting | bytes 3145728 | tf_op jit(solution)/shard_map/reshape | solution.py:52
  110.3 5.6 %fusion = f32[384,2,704]{0,2,1:T(8,128)S(1)} fusion(bf16[384,2048,1]{1,0,2:T(8,128)(2,1)} %reshape.118, bf16[1,2048,2,704]{1,3,2,0:T(8,128)(2,1)} %param.15), kind=kOutput, calls=%fused_computation.3 | convolution fusion | flops 2214592512 | bytes 9502720 | tf_op jit(solution)/shard_map/rd,dgf->rgf/dot_general | solution.py:53
  116.0 2.7 %fusion.4 = bf16[384,2048]{1,0:T(8,128)(2,1)} fusion(bf16[1,704,2048]{2,1,0:T(8,128)(2,1)S(1)} %copy-done, f32[384,2,704]{0,2,1:T(8,128)S(1)} %fusion), kind=kOutput, calls=%fused_computation.7 | convolution fusion | flops 1109704704 | bytes 6619136 | tf_op jit(solution)/shard_map/dot_general | solution.py:57
  118.6 3.6 %reshape.87 = bf16[8,4,12,2048]{3,2,1,0:T(8,128)(2,1)} reshape(bf16[384,2048]{1,0:T(8,128)(2,1)} %fusion.4) | data formatting | bytes 3145728 | tf_op jit(solution)/shard_map/reshape | solution.py:60
  122.2 4.0 %copy.30 = bf16[8,4,12,2048]{3,1,2,0:T(4,128)(2,1)} copy(bf16[8,4,12,2048]{3,2,1,0:T(8,128)(2,1)} %reshape.87) | data formatting | bytes 3145728 | tf_op jit(solution)/shard_map/reshape | solution.py:60
  126.2 12.3 %all-to-all-start.1 = ((bf16[8,4,12,2048]{3,1,2,0:T(4,128)(2,1)}), bf16[8,4,12,2048]{3,1,2,0:T(4,128)(2,1)}, u32[]{:S(2)}, u32[]{:S(2)}) async-start(bf16[8,4,12,2048]{3,1,2,0:T(4,128)(2,1)} %copy.30), calls=%async_computation.1 | async-start | bytes 3145728 | tf_op jit(solution)/shard_map/all_to_all | solution.py:107
  139.4 36.9 %all-to-all-done.1 = bf16[8,4,12,2048]{3,1,2,0:T(4,128)(2,1)} async-done(((bf16[8,4,12,2048]{3,1,2,0:T(4,128)(2,1)}), bf16[8,4,12,2048]{3,1,2,0:T(4,128)(2,1)}, u32[]{:S(2)}, u32[]{:S(2)}) %all-to-all-start.1) | async-done | bytes 1572896 | tf_op jit(solution)/shard_map/all_to_all | solution.py:107
  176.2 3.4 %copy.31 = bf16[8,4,12,2048]{3,0,2,1:T(8,128)(2,1)} copy(bf16[8,4,12,2048]{3,1,2,0:T(4,128)(2,1)} %all-to-all-done.1) | data formatting | bytes 3145728 | tf_op jit(solution)/shard_map/all_to_all | solution.py:107
  179.7 4.5 %all-to-all-start.2 = ((bf16[8,4,12,2048]{3,0,2,1:T(8,128)(2,1)}), bf16[8,4,12,2048]{3,0,2,1:T(8,128)(2,1)}, u32[]{:S(2)}, u32[]{:S(2)}) async-start(bf16[8,4,12,2048]{3,0,2,1:T(8,128)(2,1)} %copy.31), calls=%async_computation.2 | async-start | bytes 3145728 | tf_op jit(solution)/shard_map/all_to_all | solution.py:106
  184.7 2.8 %fusion.15 = f32[128,2,352]{0,2,1:T(8,128)S(1)} fusion(bf16[2048,2,352]{0,2,1:T(8,128)(2,1)} %param.13, bf16[128,2048]{1,0:T(8,128)(2,1)S(1)} %fusion.10), kind=kOutput, calls=%fused_computation.18 | convolution fusion | flops 369098752 | bytes 3768320 | tf_op jit(solution)/shard_map/td,dgf->tgf/dot_general | solution.py:88
  189.0 15.3 %all-to-all-done.2 = bf16[8,4,12,2048]{3,0,2,1:T(8,128)(2,1)} async-done(((bf16[8,4,12,2048]{3,0,2,1:T(8,128)(2,1)}), bf16[8,4,12,2048]{3,0,2,1:T(8,128)(2,1)}, u32[]{:S(2)}, u32[]{:S(2)}) %all-to-all-start.2) | async-done | bytes 1572896 | tf_op jit(solution)/shard_map/all_to_all | solution.py:106
  204.3 3.7 %copy.32 = bf16[8,4,12,2048]{3,2,1,0:T(8,128)(2,1)} copy(bf16[8,4,12,2048]{3,0,2,1:T(8,128)(2,1)} %all-to-all-done.2) | data formatting | bytes 3145728 | tf_op jit(solution)/shard_map/all_to_all | solution.py:106
  208.0 3.6 %reshape.88 = bf16[384,2048]{1,0:T(8,128)(2,1)} reshape(bf16[8,4,12,2048]{3,2,1,0:T(8,128)(2,1)} %copy.32) | data formatting | bytes 3145728 | tf_op jit(solution)/shard_map/reshape | solution.py:113
  211.6 4.4 %gather_fusion.1 = bf16[192,2048]{1,0:T(8,128)(2,1)} fusion(bf16[384,2048]{1,0:T(8,128)(2,1)} %reshape.88, s32[1024]{0:T(1024)S(1)} %pad_clamp_fusion), kind=kCustom, calls=%fused_computation.1 | custom fusion | bytes 1573632 | tf_op jit(solution)/shard_map/gather | solution.py:113
  216.0 2.2 reshape.89
  219.9 1.7 fusion.17
  222.3 21.5 %reduce-scatter.2.cloned.1.call-done = f32[128,512]{1,0:T(8,128)} async-done(((f32[128,2048]{1,0:T(8,128)}), f32[128,512]{1,0:T(8,128)}) %reduce-scatter.2.cloned.1.call-update) | async-done | bytes 262160 | tf_op jit(solution)/shard_map/reduce_scatter | solution.py:117
  243.8 1.7 select_convert_fusion
  (51 shorter events, 20.3 us)
Async XLA Ops:
  6.5 109.4 %copy-start = (bf16[1,704,2048]{2,1,0:T(8,128)(2,1)S(1)}, bf16[1,704,2048]{2,1,0:T(8,128)(2,1)}, u32[]{:S(2)}) copy-start(bf16[1,704,2048]{2,1,0:T(8,128)(2,1)} %param.16) | copy-start | bytes 8650756
  31.0 8.6 %collective-permute-start = (bf16[1,4,12,2048]{3,2,1,0:T(8,128)(2,1)S(1)}, bf16[1,4,12,2048]{3,2,1,0:T(8,128)(2,1)S(1)}, u32[]{:S(2)}, u32[]{:S(2)}) collective-permute-start(bf16[1,4,12,2048]{3,2,1,0:T(8,128)(2,1)S(1)} %get-tuple-element.13), channel_id=1, source_target_pairs={{0,4},{4,0},{8,12},{12,8},{16,20},{20,16},{24,28},{28,24},{1,5},{5... | collective-permute-start | bytes 589832 | tf_op jit(solution)/shard_map/ppermute | solution.py:25
  32.5 19.5 %collective-permute-start.1 = (bf16[1,4,12,2048]{3,2,1,0:T(8,128)(2,1)S(1)}, bf16[1,4,12,2048]{3,2,1,0:T(8,128)(2,1)S(1)}, u32[]{:S(2)}, u32[]{:S(2)}) collective-permute-start(bf16[1,4,12,2048]{3,2,1,0:T(8,128)(2,1)S(1)} %get-tuple-element.12), channel_id=1, source_target_pairs={{0,8},{4,12},{8,0},{12,4},{16,24},{20,28},{24,16},{28,20},{1,9},{5... | collective-permute-start | bytes 589832 | tf_op jit(solution)/shard_map/ppermute | solution.py:25
  34.1 22.2 %collective-permute-start.2 = (bf16[1,4,12,2048]{3,2,1,0:T(8,128)(2,1)S(1)}, bf16[1,4,12,2048]{3,2,1,0:T(8,128)(2,1)S(1)}, u32[]{:S(2)}, u32[]{:S(2)}) collective-permute-start(bf16[1,4,12,2048]{3,2,1,0:T(8,128)(2,1)S(1)} %get-tuple-element.11), channel_id=1, source_target_pairs={{0,12},{4,8},{8,4},{12,0},{16,28},{20,24},{24,20},{28,16},{1,13},{... | collective-permute-start | bytes 589832 | tf_op jit(solution)/shard_map/ppermute | solution.py:25
  34.5 22.5 %collective-permute-start.3 = (bf16[1,4,12,2048]{3,2,1,0:T(8,128)(2,1)S(1)}, bf16[1,4,12,2048]{3,2,1,0:T(8,128)(2,1)S(1)}, u32[]{:S(2)}, u32[]{:S(2)}) collective-permute-start(bf16[1,4,12,2048]{3,2,1,0:T(8,128)(2,1)S(1)} %get-tuple-element.10), channel_id=1, source_target_pairs={{0,16},{4,20},{8,24},{12,28},{16,0},{20,4},{24,8},{28,12},{1,17},{... | collective-permute-start | bytes 589832 | tf_op jit(solution)/shard_map/ppermute | solution.py:25
  37.1 36.6 %collective-permute-start.4 = (bf16[1,4,12,2048]{3,2,1,0:T(8,128)(2,1)S(1)}, bf16[1,4,12,2048]{3,2,1,0:T(8,128)(2,1)S(1)}, u32[]{:S(2)}, u32[]{:S(2)}) collective-permute-start(bf16[1,4,12,2048]{3,2,1,0:T(8,128)(2,1)S(1)} %get-tuple-element.9), channel_id=1, source_target_pairs={{0,20},{4,16},{8,28},{12,24},{16,4},{20,0},{24,12},{28,8},{1,21},{... | collective-permute-start | bytes 589832 | tf_op jit(solution)/shard_map/ppermute | solution.py:25
  39.6 34.8 %collective-permute-start.5 = (bf16[1,4,12,2048]{3,2,1,0:T(8,128)(2,1)S(1)}, bf16[1,4,12,2048]{3,2,1,0:T(8,128)(2,1)S(1)}, u32[]{:S(2)}, u32[]{:S(2)}) collective-permute-start(bf16[1,4,12,2048]{3,2,1,0:T(8,128)(2,1)S(1)} %get-tuple-element.8), channel_id=1, source_target_pairs={{0,24},{4,28},{8,16},{12,20},{16,8},{20,12},{24,0},{28,4},{1,25},{... | collective-permute-start | bytes 589832 | tf_op jit(solution)/shard_map/ppermute | solution.py:25
  52.0 23.1 %collective-permute-start.6 = (bf16[1,4,12,2048]{3,2,1,0:T(8,128)(2,1)S(1)}, bf16[1,4,12,2048]{3,2,1,0:T(8,128)(2,1)S(1)}, u32[]{:S(2)}, u32[]{:S(2)}) collective-permute-start(bf16[1,4,12,2048]{3,2,1,0:T(8,128)(2,1)S(1)} %get-tuple-element.7), channel_id=1, source_target_pairs={{0,28},{4,24},{8,20},{12,16},{16,12},{20,8},{24,4},{28,0},{1,29},{... | collective-permute-start | bytes 589832 | tf_op jit(solution)/shard_map/ppermute | solution.py:25
  126.2 50.1 %all-to-all-start.1 = ((bf16[8,4,12,2048]{3,1,2,0:T(4,128)(2,1)}), bf16[8,4,12,2048]{3,1,2,0:T(4,128)(2,1)}, u32[]{:S(2)}, u32[]{:S(2)}) async-start(bf16[8,4,12,2048]{3,1,2,0:T(4,128)(2,1)} %copy.30), calls=%async_computation.1 | async-start | bytes 3145728 | tf_op jit(solution)/shard_map/all_to_all | solution.py:107
  179.7 4.6 %copy-start.3 = (s32[32]{0:T(128)S(1)}, s32[32]{0:T(128)}, u32[]{:S(2)}) copy-start(s32[32]{0:T(128)} %param.17) | copy-start | bytes 388
  179.7 24.6 %all-to-all-start.2 = ((bf16[8,4,12,2048]{3,0,2,1:T(8,128)(2,1)}), bf16[8,4,12,2048]{3,0,2,1:T(8,128)(2,1)}, u32[]{:S(2)}, u32[]{:S(2)}) async-start(bf16[8,4,12,2048]{3,0,2,1:T(8,128)(2,1)} %copy.31), calls=%async_computation.2 | async-start | bytes 3145728 | tf_op jit(solution)/shard_map/all_to_all | solution.py:106
  184.2 59.6 %reduce-scatter.2.cloned.1.call-start = ((), (), s32[]{:S(2)}) async-start(), calls=%async_computation.4 | async-start | bytes 1310720 | tf_op jit(solution)/shard_map/reduce_scatter | solution.py:117
  184.7 2.9 %copy-start.1 = (bf16[352,2048]{1,0:T(8,128)(2,1)S(1)}, bf16[352,2048]{1,0:T(8,128)(2,1)}, u32[]{:S(2)}) copy-start(bf16[352,2048]{1,0:T(8,128)(2,1)} %param.14) | copy-start | bytes 4325380
  216.0 27.8 %copy-start.2 = (bf16[128,512]{1,0:T(8,128)(2,1)S(1)}, bf16[128,512]{1,0:T(8,128)(2,1)}, u32[]{:S(2)}) copy-start(bf16[128,512]{1,0:T(8,128)(2,1)} %param.10) | copy-start | bytes 393220
Sparse Core Ops, SparseCore 0:
  221.8 21.9 reduce-scatter.1
